TPU v7x, 32 devices: a whole 2x2x4 slice. The times are simulated.
32 devices in a mesh: seq: 4 (over x, core), span: 8 (over z, y).
Axes of the slice: x: 2, y: 2, z: 4, core: 2. Of those that a mesh axis runs over, the one named last changes fastest.
Arguments:
- llm_input: bfloat16 [512, 5120], P(('seq', 'span')), may hold values from -6 to 6
- hidden_grad: bfloat16 [512, 32768], P(None, ('seq', 'span')), may hold values from -1.5 to 1.5
- gate_act: bfloat16 [512, 32768], P(None, ('seq', 'span')), may hold values from -6 to 6
- up_weight: bfloat16 [5120, 32768], P(None, ('seq', 'span')), may hold values from -0.078125 to 0.078125
- span_counts: int32 [16], replicated, may hold values from 16 to 48, as said below
- row_ticks: int32 [512], replicated, may hold values from 0 to 47, as said below
- encoder_out: bfloat16 [8, 384, 1280], P('span'), may hold values from -6 to 6
- mlp_input: bfloat16 [8, 384, 1280], P('span'), may hold values from -6 to 6
- post_gain: float32 [1280], replicated, may hold values from 0.5 to 1.5
- post_bias: float32 [1280], replicated, may hold values from -3 to 3
- adapter_in: bfloat16 [5120, 5120], P(None, 'seq'), may hold values from -0.078125 to 0.078125
- adapter_out: bfloat16 [5120, 5120], P('seq'), may hold values from -0.078125 to 0.078125
- expand_weight: bfloat16 [1280, 5120], P(None, 'seq'), may hold values from -0.15625 to 0.15625
- expand_bias: float32 [5120], P('seq'), may hold values from -3 to 3
- contract_weight: bfloat16 [5120, 1280], P('seq'), may hold values from -0.078125 to 0.078125
Outputs:
- gate_act_grad: bfloat16 [512, 32768], P(None, ('seq', 'span'))
- up_weight_grad: bfloat16 [5120, 32768], P(None, ('seq', 'span'))
- adapter_in_grad: bfloat16 [5120, 5120], P('span', 'seq')
- adapter_out_grad: bfloat16 [5120, 5120], P(('seq', 'span'))
- expand_weight_grad: bfloat16 [1280, 5120], P('span', 'seq')
- contract_weight_grad: bfloat16 [5120, 1280], P(('seq', 'span'))
- expand_bias_grad: float32 [5120], P('seq')
- post_gain_grad: float32 [1280], replicated
- post_bias_grad: float32 [1280], replicated
- contract_bias_grad: float32 [1280], replicated
- encoder_out_grad: bfloat16 [8, 384, 1280], P('span', 'seq')
- mlp_input_grad: bfloat16 [8, 384, 1280], P('span', 'seq')
Inputs may be any that keep to these rules, and one draw needn't show every extreme that they name: span_counts sums to 512; its largest entry is exactly 48. `row_ticks`: the rows of each span are consecutive in the sequence, spans in order of their number, span k holding span_counts[k] rows; inside a span the tick rises by one from row to row.
All inputs are finite; a program needn't handle non-finite values.
Results may differ from a plain program's by a relative error of at most 0.03.
Values may be sent and summed in bfloat16 or wider, within the bound.
A program may use at most 192 MiB of HBM per device.

v0:
```python
import math
import jax
import jax.numpy as jnp
from jax import lax
from jax.sharding import PartitionSpec as P

STACK = 4
CH_DEV = 2
EPSILON = 1e-05


def gelu_value(values):
    return 0.5 * values * (1.0 + lax.erf(values * (1.0 / math.sqrt(2.0))))


def gelu_slope(values):
    cumulative = 0.5 * (1.0 + lax.erf(values * (1.0 / math.sqrt(2.0))))
    return cumulative + values * jnp.exp(-0.5 * values * values) * (1.0 / math.sqrt(2.0 * math.pi))


def locate_rows(span_counts, row_ticks, capacity):
    span_ends = jnp.cumsum(span_counts)
    positions = jnp.arange(row_ticks.shape[0], dtype=jnp.int32)
    span_of = jnp.sum((positions[:, None] >= span_ends[None, :]).astype(jnp.int32), axis=1)
    return span_of * capacity + row_ticks


def contract_last(left, right):
    return lax.dot_general(
        left, right, (((1,), (1,)), ((), ())), preferred_element_type=jnp.float32
    )


def contract_first(left, right):
    return lax.dot_general(
        left, right, (((0,), (0,)), ((), ())), preferred_element_type=jnp.float32
    )


def per_device(
    llm_input,
    hidden_grad,
    gate_act,
    up_weight,
    span_counts,
    row_ticks,
    encoder_out,
    mlp_input,
    post_gain,
    post_bias,
    adapter_in,
    adapter_out,
    expand_weight,
    expand_bias,
    contract_weight,
):
    rows_all = row_ticks.shape[0]
    up_grad = (hidden_grad.astype(jnp.float32) * gate_act.astype(jnp.float32)).astype(jnp.bfloat16)
    frames_each = encoder_out.shape[1]
    width = encoder_out.shape[2]
    slots_each = frames_each // STACK
    capacity = slots_each // CH_DEV
    owner_count = lax.axis_size("span")
    slot_of = locate_rows(span_counts, row_ticks, capacity)
    total_slots = owner_count * slots_each
    matches = jnp.arange(total_slots, dtype=jnp.int32)[:, None] == slot_of[None, :]
    filled = jnp.any(matches, axis=1)
    source = jnp.sum(jnp.where(matches, jnp.arange(rows_all, dtype=jnp.int32)[None, :], 0), axis=1)
    picked = jnp.take(up_grad, source, axis=0) * filled[:, None].astype(jnp.bfloat16)
    partial_slots = lax.psum_scatter(
        contract_last(picked, up_weight).astype(jnp.bfloat16),
        "span",
        scatter_dimension=0,
        tiled=True,
    )
    token_grad = lax.psum(partial_slots, "seq")
    piece = lax.all_gather(llm_input, ("seq", "span"), axis=0, tiled=True)
    weight_sum = contract_first(piece, up_grad)
    block = jnp.dot(piece, up_weight, preferred_element_type=jnp.float32)
    up_rows = block
    weight_sum, up_rows = (weight_sum, up_rows)
    gate_act_grad = (hidden_grad.astype(jnp.float32) * up_rows).astype(jnp.bfloat16)
    up_weight_grad = weight_sum.astype(jnp.bfloat16)
    frames = encoder_out[0].astype(jnp.float32)
    centre = frames - jnp.mean(frames, axis=1, keepdims=True)
    rstd = lax.rsqrt(jnp.mean(centre * centre, axis=1, keepdims=True) + EPSILON)
    nhat = centre * rstd
    stacked = (nhat * post_gain + post_bias).reshape(slots_each, STACK * width).astype(jnp.bfloat16)
    pre_act = jnp.dot(stacked, adapter_in, preferred_element_type=jnp.float32)
    activity = gelu_value(pre_act).astype(jnp.bfloat16)
    act_grad = contract_last(token_grad, adapter_out)
    pre_grad = (act_grad * gelu_slope(pre_act)).astype(jnp.bfloat16)
    partial_out = contract_first(activity, token_grad)
    partial_in = contract_first(stacked, pre_grad)
    adapter_in_sum, adapter_out_sum = (
        lax.psum_scatter(
            partial_in.astype(jnp.bfloat16), "span", scatter_dimension=0, tiled=True
        ).astype(jnp.float32),
        lax.psum_scatter(
            partial_out.astype(jnp.bfloat16), "span", scatter_dimension=0, tiled=True
        ).astype(jnp.float32),
    )
    stacked_part = contract_last(pre_grad, adapter_in)
    mine_frames = frames_each // lax.axis_size("seq")
    seq_index = lax.axis_index("seq")
    normed_grad = (
        lax.psum(stacked_part.astype(jnp.bfloat16), "seq")
        .astype(jnp.float32)
        .reshape(frames_each, width)
    )
    scaled = normed_grad * post_gain
    resid = rstd * (
        scaled
        - jnp.mean(scaled, axis=1, keepdims=True)
        - nhat * jnp.mean(scaled * nhat, axis=1, keepdims=True)
    )
    resid = resid.astype(jnp.bfloat16)
    gain_part = jnp.sum(normed_grad * nhat, axis=0)
    shift_part = jnp.sum(normed_grad, axis=0)
    out_bias_part = jnp.sum(resid.astype(jnp.float32), axis=0)
    resid_mine = lax.dynamic_slice_in_dim(resid, seq_index * mine_frames, mine_frames, 0)
    inputs = mlp_input[0]
    hidden_pre = jnp.dot(inputs, expand_weight, preferred_element_type=jnp.float32) + expand_bias
    hidden_act = gelu_value(hidden_pre).astype(jnp.bfloat16)
    hidden_enc_grad = contract_last(resid, contract_weight)
    hidden_pre_grad = (hidden_enc_grad * gelu_slope(hidden_pre)).astype(jnp.bfloat16)
    partial_expand = contract_first(inputs, hidden_pre_grad)
    partial_contract = contract_first(hidden_act, resid)
    expand_sum, contract_sum = (
        lax.psum_scatter(
            partial_expand.astype(jnp.bfloat16), "span", scatter_dimension=0, tiled=True
        ).astype(jnp.float32),
        lax.psum_scatter(
            partial_contract.astype(jnp.bfloat16), "span", scatter_dimension=0, tiled=True
        ).astype(jnp.float32),
    )
    in_bias_part = jnp.sum(hidden_pre_grad.astype(jnp.float32), axis=0)
    mlp_part = contract_last(hidden_pre_grad, expand_weight)
    mlp_input_grad = lax.psum_scatter(
        mlp_part.astype(jnp.bfloat16), "seq", scatter_dimension=0, tiled=True
    )
    expand_bias_grad, post_gain_grad, post_bias_grad, contract_bias_grad = lax.psum(
        (in_bias_part, gain_part, shift_part, out_bias_part), "span"
    )
    return (
        gate_act_grad,
        up_weight_grad,
        adapter_in_sum.astype(jnp.bfloat16),
        adapter_out_sum.astype(jnp.bfloat16),
        expand_sum.astype(jnp.bfloat16),
        contract_sum.astype(jnp.bfloat16),
        expand_bias_grad,
        post_gain_grad,
        post_bias_grad,
        contract_bias_grad,
        resid_mine.reshape(1, mine_frames, width),
        mlp_input_grad.reshape(1, mine_frames, width),
    )


def solution(mesh):
    return jax.shard_map(
        per_device,
        mesh=mesh,
        in_specs=(
            P(("seq", "span"), None),
            P(None, ("seq", "span")),
            P(None, ("seq", "span")),
            P(None, ("seq", "span")),
            P(),
            P(),
            P("span", None, None),
            P("span", None, None),
            P(),
            P(),
            P(None, "seq"),
            P("seq", None),
            P(None, "seq"),
            P("seq"),
            P("seq", None),
        ),
        out_specs=(
            P(None, ("seq", "span")),
            P(None, ("seq", "span")),
            P("span", "seq"),
            P(("seq", "span"), None),
            P("span", "seq"),
            P(("seq", "span"), None),
            P("seq"),
            P(),
            P(),
            P(),
            P("span", "seq", None),
            P("span", "seq", None),
        ),
        check_vma=False,
    )
```

profile of v0, /device:TPU:0, one launch (start us, length us, event | category | flops | bytes accessed | tf_op | source)
XLA Modules:
  0.0 915.3 jit_solution(14220045984964570281)
XLA Ops:
  10.4 2.9 fusion.7
  13.3 5.9 gather_fusion
  19.2 13.5 %convolution_convert_fusion.2 = bf16[768,5120]{1,0:T(8,128)(2,1)} fusion(bf16[5120,1024]{1,0:T(8,128)(2,1)} %param.18, bf16[768,1024]{1,0:T(8,128)(2,1)} %gather_fusion, pred[768]{0:T(1024)(128)(4,1)S(1)} %compare_and_fusion, bf16[768]{0:T(1024)(128)(2,1)S(1)} %convert_element_type.111), kind=kOutput, calls=%fused_computation.4 | convolution fusion | flops 8058568704 | bytes 19925248 | tf_op jit(solution)/shard_map/dot_general | solution.py:29
  42.8 4.2 add_convert_fusion
  47.0 128.9 %reduce-scatter.9.cloned.1.call-done = bf16[96,5120]{1,0:T(8,128)(2,1)} async-done(((bf16[768,5120]{1,0:T(8,128)(2,1)}), bf16[96,5120]{1,0:T(8,128)(2,1)}) %reduce-scatter.9.cloned.1.call-update) | async-done | bytes 983056 | tf_op jit(solution)/shard_map/reduce_scatter | solution.py:70
  176.1 8.0 fusion.37
  184.1 29.1 %all-reduce.4.cloned.1.call-done = bf16[96,5120]{1,0:T(8,128)(2,1)} async-done(((bf16[96,5120]{1,0:T(8,128)(2,1)}), bf16[96,5120]{1,0:T(8,128)(2,1)}) %all-reduce.4.cloned.1.call-update) | async-done | bytes 983056 | tf_op jit(solution)/shard_map/psum | solution.py:76
  213.2 9.2 %fusion.5 = bf16[96,1280]{1,0:T(8,128)(2,1)S(1)} fusion(bf16[96,5120]{1,0:T(8,128)(2,1)} %all-reduce.4.cloned.1.call-done, bf16[1280,5120]{1,0:T(8,128)(2,1)} %param.26, f32[96,1280]{1,0:T(8,128)} %fusion.37), kind=kOutput, calls=%fused_computation.23 | convolution fusion | flops 1259520000 | bytes 14827520 | tf_op jit(solution)/shard_map/dot_general | solution.py:29
  222.4 9.7 %convolution_convert_fusion.5 = bf16[96,5120]{1,0:T(8,128)(2,1)} fusion(bf16[96,1280]{1,0:T(8,128)(2,1)S(1)} %fusion.5, bf16[5120,1280]{1,0:T(8,128)(2,1)} %param.25), kind=kOutput, calls=%fused_computation.8 | convolution fusion | flops 1258782720 | bytes 14336000 | tf_op jit(solution)/shard_map/dot_general | solution.py:29
  235.5 3.9 convolution_add_fusion
  239.4 36.7 %all-reduce.6.cloned.1.call-done = bf16[384,1280]{1,0:T(8,128)(2,1)} async-done(((bf16[384,1280]{1,0:T(8,128)(2,1)}), bf16[384,1280]{1,0:T(8,128)(2,1)}) %all-reduce.6.cloned.1.call-update) | async-done | bytes 983056 | tf_op jit(solution)/shard_map/psum | solution.py:107
  280.3 3.8 convert_reduce_fusion.2
  287.5 3.4 fusion
  290.9 3.4 copy.39
  296.4 3.7 convolution_convert_fusion.3
  301.3 6.6 convolution_convert_fusion.1
  309.2 6.7 convolution_convert_fusion
  317.1 10.6 %convert_bitcast_fusion = bf16[5120,1024]{0,1:T(8,128)(2,1)} fusion(bf16[512,1024]{1,0:T(8,128)(2,1)S(1)} %copy-done.2, bf16[512,5120]{1,0:T(8,128)(2,1)} %all-gather.2.cloned.1.call-done), kind=kOutput, calls=%fused_computation.3 | convolution fusion | flops 5373952000 | bytes 16777216 | tf_op jit(solution)/shard_map/dot_general | solution.py:35
  327.7 14.5 %copy.37 = bf16[5120,1024]{1,0:T(8,128)(2,1)} copy(bf16[5120,1024]{0,1:T(8,128)(2,1)} %convert_bitcast_fusion) | data formatting | bytes 20971520
  342.2 11.0 %fusion.6 = bf16[512,1024]{1,0:T(8,128)(2,1)} fusion(bf16[512,1024]{1,0:T(8,128)(2,1)} %param.16, bf16[512,5120]{1,0:T(8,128)(2,1)} %all-gather.2.cloned.1.call-done, bf16[5120,1024]{1,0:T(8,128)(2,1)} %param.18), kind=kOutput, calls=%fused_computation.24 | convolution fusion | flops 5370281984 | bytes 17825792 | tf_op jit(solution)/shard_map/dot_general | solution.py:79
  353.2 38.6 %all-reduce = (f32[1280]{0:T(1024)}, f32[1280]{0:T(1024)}, f32[1280]{0:T(1024)}, f32[1280]{0:T(1024)}) all-reduce(f32[1280]{0:T(1024)S(1)} %get-tuple-element.70, f32[1280]{0:T(1024)S(1)} %get-tuple-element.60, f32[1280]{0:T(1024)S(1)} %get-tuple-element.63, f32[1280]{0:T(1024)S(1)} %copy-done.11), channel_id=1, replica_groups=mesh['seq'=4,'span'=8] {'span'}, use_global_device_ids=true, to_apply=%region_16.17 | all-reduce | flops 5120 | bytes 40960 | tf_op jit(solution)/shard_map/psum | solution.py:142
  393.4 77.9 %reduce-scatter.15.cloned.1.call-done = bf16[160,1280]{1,0:T(8,128)(2,1)} async-done(((bf16[1280,1280]{1,0:T(8,128)(2,1)}), bf16[160,1280]{1,0:T(8,128)(2,1)}) %reduce-scatter.15.cloned.1.call-update) | async-done | bytes 409616 | tf_op jit(solution)/shard_map/reduce_scatter | solution.py:133
  471.3 218.4 %reduce-scatter.11.cloned.1.call-done = bf16[640,1280]{1,0:T(8,128)(2,1)} async-done(((bf16[5120,1280]{1,0:T(8,128)(2,1)}), bf16[640,1280]{1,0:T(8,128)(2,1)}) %reduce-scatter.11.cloned.1.call-update) | async-done | bytes 1638416 | tf_op jit(solution)/shard_map/reduce_scatter | solution.py:96
  689.7 218.1 %reduce-scatter.13.cloned.1.call-done = bf16[160,5120]{1,0:T(8,128)(2,1)} async-done(((bf16[1280,5120]{1,0:T(8,128)(2,1)}), bf16[160,5120]{1,0:T(8,128)(2,1)}) %reduce-scatter.13.cloned.1.call-update) | async-done | bytes 1638416 | tf_op jit(solution)/shard_map/reduce_scatter | solution.py:99
  (87 shorter events, 30.8 us)
Async XLA Ops:
  8.0 227.5 %copy-start = (bf16[1280,1280]{1,0:T(8,128)(2,1)S(1)}, bf16[1280,1280]{1,0:T(8,128)(2,1)}, u32[]{:S(2)}) copy-start(bf16[1280,1280]{1,0:T(8,128)(2,1)} %param.27) | copy-start | bytes 9830404
  8.0 167.8 %reduce-scatter.9.cloned.1.call-start = ((), (), s32[]{:S(2)}) async-start(), calls=%async_computation.7 | async-start | bytes 8847360 | tf_op jit(solution)/shard_map/reduce_scatter | solution.py:70
  32.8 180.4 %all-reduce.4.cloned.1.call-start = ((), (), s32[]{:S(2)}) async-start(), calls=%async_computation.8 | async-start | bytes 1966080 | tf_op jit(solution)/shard_map/psum | solution.py:76
  41.0 1.7 copy-start.12
  41.0 1.7 copy-start.10
  175.9 100.3 %all-reduce.6.cloned.1.call-start = ((), (), s32[]{:S(2)}) async-start(), calls=%async_computation.11 | async-start | bytes 1966080 | tf_op jit(solution)/shard_map/psum | solution.py:107
  232.2 3.4 copy-start.13
  234.7 81.3 %all-gather.2.cloned.1.call-start = ((), (), s32[]{:S(2)}) async-start(), calls=%async_computation.6 | async-start | bytes 5406720 | tf_op jit(solution)/shard_map/all_gather | solution.py:77
  235.2 158.2 %reduce-scatter.17.cloned.1.call-start = ((), (), s32[]{:S(2)}) async-start(), calls=%async_computation.13 | async-start | bytes 1228800 | tf_op jit(solution)/shard_map/reduce_scatter | solution.py:139
  276.1 2.6 copy-start.3
  276.1 2.6 copy-start.7
  278.7 1.6 copy-start.14
  280.1 3.9 copy-start.8
  287.5 106.0 %reduce-scatter.19.cloned.1.call-start = ((), (), s32[]{:S(2)}) async-start(), calls=%async_computation.14 | async-start | bytes 3686400
  294.4 1.3 copy-start.9
  294.4 2.0 copy-start.15
  294.4 176.9 %reduce-scatter.15.cloned.1.call-start = ((), (), s32[]{:S(2)}) async-start(), calls=%async_computation.12 | async-start | bytes 3686400 | tf_op jit(solution)/shard_map/reduce_scatter | solution.py:133
  300.1 1.2 copy-start.4
  300.1 389.6 %reduce-scatter.11.cloned.1.call-start = ((), (), s32[]{:S(2)}) async-start(), calls=%async_computation.9 | async-start | bytes 14745600 | tf_op jit(solution)/shard_map/reduce_scatter | solution.py:96
  307.8 1.4 copy-start.6
  307.9 599.9 %reduce-scatter.13.cloned.1.call-start = ((), (), s32[]{:S(2)}) async-start(), calls=%async_computation.10 | async-start | bytes 14745600 | tf_op jit(solution)/shard_map/reduce_scatter | solution.py:99
  315.9 1.2 copy-start.2
  342.2 11.0 %copy-start.11 = (f32[1280]{0:T(1024)S(1)}, f32[1280]{0:T(1024)}, u32[]{:S(2)}) copy-start(f32[1280]{0:T(1024)} %get-tuple-element.68) | copy-start | bytes 15364
  342.2 565.6 %copy-start.1 = (bf16[1280,1280]{1,0:T(8,128)(2,1)S(1)}, bf16[1280,1280]{1,0:T(8,128)(2,1)}, u32[]{:S(2)}) copy-start(bf16[1280,1280]{1,0:T(8,128)(2,1)} %param.27) | copy-start | bytes 9830404
  (2 other events, 2.0 us)
Sparse Core Ops, SparseCore 0:
  32.9 142.9 reduce-scatter.8
  178.2 34.9 all-reduce.3
  234.8 41.3 all-reduce.5
  287.6 24.4 reduce-scatter.16
  316.1 76.0 reduce-scatter.18
  396.2 75.0 reduce-scatter.14
  475.6 214.0 reduce-scatter.10
  693.9 213.8 reduce-scatter.12
Sparse Core Ops, SparseCore 1:
  238.0 67.4 all-gather.1
where the time goes:
time: 916 us; the launch traced here: 915 us
  waiting for transfers between devices  710 us (78%)
  matrix products  92.6 us (10%)
  local copies, waits for them, and re-layouts  42 us (5%)
  blocking collectives  38.6 us (4%)
  between operations  15.8 us (2%)
  other arithmetic  15.5 us (2%)
    reduce_scatter x1, waiting for transfers between devices, per_device(): lax.psum_scatter(partial_in.astype(jnp.bfloat16), 'span', scatter_dimensi...  218 us
    reduce_scatter x1, waiting for transfers between devices, per_device(): lax.psum_scatter(partial_out.astype(jnp.bfloat16), 'span', scatter_dimens...  218 us
    reduce_scatter x1, waiting for transfers between devices, per_device(): lax.psum_scatter(contract_last(picked, up_weight).astype(jnp.bfloat16), '...  129 us
    reduce_scatter x1, waiting for transfers between devices, per_device(): lax.psum_scatter(partial_contract.astype(jnp.bfloat16), 'span', scatter_d...  77.9 us
    dot_general x5, matrix products, contract_last(): lax.dot_general(left, right, (((1,), (1,)), ((), ())), preferred_element_...  38.7 us
    psum x1, blocking collectives, per_device(): lax.psum((in_bias_part, gain_part, shift_part, out_bias_part), 'span')  38.6 us
    psum x1, waiting for transfers between devices, per_device(): lax.psum(stacked_part.astype(jnp.bfloat16), 'seq').astype(jnp.float32)  36.7 us
    dot_general x5, matrix products, contract_first(): lax.dot_general(left, right, (((0,), (0,)), ((), ())), preferred_element_...  31 us
  transfers between devices with their start and end apart: 9, of which 6 were waited for; matrix products, arithmetic and copies ran while one was open for 11% of the time, Pallas kernels for 0%

commit v1 on v0

--- a/solution.py
+++ b/solution.py
@@ -1,12 +1,21 @@
+import functools
 import math
 import jax
 import jax.numpy as jnp
 from jax import lax
 from jax.sharding import PartitionSpec as P
+from jax.lax import all_gather
 
 STACK = 4
 CH_DEV = 2
 EPSILON = 1e-05
+
+
+def recover_masks(body, along_axis):
+    return jnp.sum(all_gather(body, along_axis), axis=0)
+
+
+step_on_local_data = functools.partial(recover_masks, along_axis="seq")
 
 
 def gelu_value(values):
@@ -104,7 +113,7 @@
     mine_frames = frames_each // lax.axis_size("seq")
     seq_index = lax.axis_index("seq")
     normed_grad = (
-        lax.psum(stacked_part.astype(jnp.bfloat16), "seq")
+        step_on_local_data(stacked_part.astype(jnp.bfloat16))
         .astype(jnp.float32)
         .reshape(frames_each, width)
     )

time: 916 us -> 963 us (1.051)
  waiting for transfers between devices: 710 us -> 756 us
    psum x1 -> x0, waiting for transfers between devices: 36.7 us -> none  [per_device(): lax.psum(stacked_part.astype(jnp.bfloat16), 'seq').astype(jnp.float32)]
    unnamed x10, waiting for transfers between devices: 0.65 us -> 32.7 us
    all_gather x0 -> x1, waiting for transfers between devices: none -> 28.7 us  [recover_masks(): return jnp.sum(all_gather(body, along_axis), axis=0)]
    all_gather x1, waiting for transfers between devices: 0.03 us -> 21.5 us  [per_device(): piece = lax.all_gather(llm_input, ('seq', 'span'), axis=0, tiled=True)]
  transfers between devices with their start and end apart: 9 -> 9, of which waited for: 6 -> 8; matrix products, arithmetic and copies ran while one was open for 11% -> 11% of each run, Pallas kernels for 0% -> 0%
where the time goes in v1:
time: 963 us; the launch traced here: 962 us
  waiting for transfers between devices  756 us (79%)
  matrix products  92 us (10%)
  local copies, waits for them, and re-layouts  41.4 us (4%)
  blocking collectives  37.4 us (4%)
  other arithmetic  19.7 us (2%)
  between operations  14.1 us (1%)
    reduce_scatter x1, waiting for transfers between devices, per_device(): lax.psum_scatter(partial_in.astype(jnp.bfloat16), 'span', scatter_dimensi...  218 us
    reduce_scatter x1, waiting for transfers between devices, per_device(): lax.psum_scatter(partial_out.astype(jnp.bfloat16), 'span', scatter_dimens...  218 us
    reduce_scatter x1, waiting for transfers between devices, per_device(): lax.psum_scatter(contract_last(picked, up_weight).astype(jnp.bfloat16), '...  129 us
    reduce_scatter x1, waiting for transfers between devices, per_device(): lax.psum_scatter(partial_contract.astype(jnp.bfloat16), 'span', scatter_d...  79.1 us
    dot_general x5, matrix products, contract_last(): lax.dot_general(left, right, (((1,), (1,)), ((), ())), preferred_element_...  38.2 us
    psum x1, blocking collectives, per_device(): lax.psum((in_bias_part, gain_part, shift_part, out_bias_part), 'span')  37.4 us
    unnamed x10, waiting for transfers between devices  32.7 us
    dot_general x5, matrix products, contract_first(): lax.dot_general(left, right, (((0,), (0,)), ((), ())), preferred_element_...  31 us
  transfers between devices with their start and end apart: 9, of which 8 were waited for; matrix products, arithmetic and copies ran while one was open for 11% of the time, Pallas kernels for 0%

profile of v1, /device:TPU:0, one launch (start us, length us, event | category | flops | bytes accessed | tf_op | source)
XLA Modules:
  0.0 962.0 jit_solution(16226346290992361996)
XLA Ops:
  12.5 5.9 gather_fusion
  18.4 13.5 %convolution_convert_fusion.2 = bf16[768,5120]{1,0:T(8,128)(2,1)} fusion(bf16[5120,1024]{1,0:T(8,128)(2,1)} %param.18, bf16[768,1024]{1,0:T(8,128)(2,1)} %gather_fusion, pred[768]{0:T(1024)(128)(4,1)S(1)} %compare_and_fusion, bf16[768]{0:T(1024)(128)(2,1)S(1)} %convert_element_type.119), kind=kOutput, calls=%fused_computation.4 | convolution fusion | flops 8058568704 | bytes 19925248 | tf_op jit(solution)/shard_map/dot_general | solution.py:38
  41.9 4.2 add_convert_fusion
  46.1 128.9 %reduce-scatter.9.cloned.1.call-done = bf16[96,5120]{1,0:T(8,128)(2,1)} async-done(((bf16[768,5120]{1,0:T(8,128)(2,1)}), bf16[96,5120]{1,0:T(8,128)(2,1)}) %reduce-scatter.9.cloned.1.call-update) | async-done | bytes 983056 | tf_op jit(solution)/shard_map/reduce_scatter | solution.py:79
  175.3 8.0 fusion.28
  183.3 29.1 %all-reduce.3.cloned.1.call-done = bf16[96,5120]{1,0:T(8,128)(2,1)} async-done(((bf16[96,5120]{1,0:T(8,128)(2,1)}), bf16[96,5120]{1,0:T(8,128)(2,1)}) %all-reduce.3.cloned.1.call-update) | async-done | bytes 983056 | tf_op jit(solution)/shard_map/psum | solution.py:85
  212.4 9.2 fusion.2
  221.6 9.7 %convolution_convert_fusion.5 = bf16[96,5120]{1,0:T(8,128)(2,1)} fusion(bf16[96,1280]{1,0:T(8,128)(2,1)S(1)} %fusion.2, bf16[5120,1280]{1,0:T(8,128)(2,1)} %param.25), kind=kOutput, calls=%fused_computation.8 | convolution fusion | flops 1258782720 | bytes 14336000 | tf_op jit(solution)/shard_map/dot_general | solution.py:38
  232.2 3.9 convolution_add_fusion
  236.1 28.7 %all-gather.6.cloned.1.call-done = bf16[384,5120]{1,0:T(8,128)(2,1)} async-done(((bf16[96,5120]{1,0:T(8,128)(2,1)}), bf16[384,5120]{1,0:T(8,128)(2,1)}) %all-gather.6.cloned.1.call-update) | async-done | bytes 3932176 | tf_op jit(solution)/shard_map/all_gather | solution.py:15
  264.8 4.0 reduce_sum.109
  286.5 3.4 copy.39
  291.8 3.7 convolution_convert_fusion.3
  296.7 6.6 convolution_convert_fusion.1
  304.7 6.7 convolution_convert_fusion
  311.4 21.5 %all-gather.4.cloned.1.call-done = bf16[512,5120]{1,0:T(8,128)(2,1)} async-done(((bf16[16,5120]{1,0:T(8,128)(2,1)}), bf16[512,5120]{1,0:T(8,128)(2,1)}) %all-gather.4.cloned.1.call-update) | async-done | bytes 5242896 | tf_op jit(solution)/shard_map/all_gather | solution.py:86
  332.9 10.6 %convert_bitcast_fusion = bf16[5120,1024]{0,1:T(8,128)(2,1)} fusion(bf16[512,1024]{1,0:T(8,128)(2,1)S(1)} %copy-done.2, bf16[512,5120]{1,0:T(8,128)(2,1)} %all-gather.4.cloned.1.call-done), kind=kOutput, calls=%fused_computation.3 | convolution fusion | flops 5373952000 | bytes 16777216 | tf_op jit(solution)/shard_map/dot_general | solution.py:44
  343.5 14.4 %copy.37 = bf16[5120,1024]{1,0:T(8,128)(2,1)} copy(bf16[5120,1024]{0,1:T(8,128)(2,1)} %convert_bitcast_fusion) | data formatting | bytes 20971520
  357.9 10.9 %fusion.3 = bf16[512,1024]{1,0:T(8,128)(2,1)} fusion(bf16[512,1024]{1,0:T(8,128)(2,1)} %param.16, bf16[512,5120]{1,0:T(8,128)(2,1)} %all-gather.4.cloned.1.call-done, bf16[5120,1024]{1,0:T(8,128)(2,1)} %param.18), kind=kOutput, calls=%fused_computation.18 | convolution fusion | flops 5370281984 | bytes 17825792 | tf_op jit(solution)/shard_map/dot_general | solution.py:88
  368.9 37.4 %all-reduce = (f32[1280]{0:T(1024)}, f32[1280]{0:T(1024)}, f32[1280]{0:T(1024)}, f32[1280]{0:T(1024)}) all-reduce(f32[1280]{0:T(1024)S(1)} %get-tuple-element.70, f32[1280]{0:T(1024)S(1)} %get-tuple-element.60, f32[1280]{0:T(1024)S(1)} %get-tuple-element.63, f32[1280]{0:T(1024)S(1)} %copy-done.11), channel_id=1, replica_groups=mesh['seq'=4,'span'=8] {'span'}, use_global_device_ids=true, to_apply=%region_16.17 | all-reduce | flops 5120 | bytes 40960 | tf_op jit(solution)/shard_map/psum | solution.py:151
  407.9 32.0 %reduce-scatter.19.cloned.1.call-done = bf16[160,1280]{1,0:T(8,128)(2,1)} async-done(((bf16[1280,1280]{1,0:T(8,128)(2,1)}), bf16[160,1280]{1,0:T(8,128)(2,1)}) %reduce-scatter.19.cloned.1.call-update) | async-done | bytes 409616
  439.9 79.1 %reduce-scatter.15.cloned.1.call-done = bf16[160,1280]{1,0:T(8,128)(2,1)} async-done(((bf16[1280,1280]{1,0:T(8,128)(2,1)}), bf16[160,1280]{1,0:T(8,128)(2,1)}) %reduce-scatter.15.cloned.1.call-update) | async-done | bytes 409616 | tf_op jit(solution)/shard_map/reduce_scatter | solution.py:142
  519.0 218.4 %reduce-scatter.11.cloned.1.call-done = bf16[640,1280]{1,0:T(8,128)(2,1)} async-done(((bf16[5120,1280]{1,0:T(8,128)(2,1)}), bf16[640,1280]{1,0:T(8,128)(2,1)}) %reduce-scatter.11.cloned.1.call-update) | async-done | bytes 1638416 | tf_op jit(solution)/shard_map/reduce_scatter | solution.py:105
  737.3 218.1 %reduce-scatter.13.cloned.1.call-done = bf16[160,5120]{1,0:T(8,128)(2,1)} async-done(((bf16[1280,5120]{1,0:T(8,128)(2,1)}), bf16[160,5120]{1,0:T(8,128)(2,1)}) %reduce-scatter.13.cloned.1.call-update) | async-done | bytes 1638416 | tf_op jit(solution)/shard_map/reduce_scatter | solution.py:108
  (88 shorter events, 40.0 us)
Async XLA Ops:
  7.2 225.0 %copy-start = (bf16[1280,1280]{1,0:T(8,128)(2,1)S(1)}, bf16[1280,1280]{1,0:T(8,128)(2,1)}, u32[]{:S(2)}) copy-start(bf16[1280,1280]{1,0:T(8,128)(2,1)} %param.27) | copy-start | bytes 9830404
  7.2 167.8 %reduce-scatter.9.cloned.1.call-start = ((), (), s32[]{:S(2)}) async-start(), calls=%async_computation.7 | async-start | bytes 8847360 | tf_op jit(solution)/shard_map/reduce_scatter | solution.py:79
  31.9 180.4 %all-reduce.3.cloned.1.call-start = ((), (), s32[]{:S(2)}) async-start(), calls=%async_computation.8 | async-start | bytes 1966080 | tf_op jit(solution)/shard_map/psum | solution.py:85
  40.2 1.7 copy-start.12
  40.2 1.7 copy-start.10
  175.0 89.8 %all-gather.6.cloned.1.call-start = ((), (), s32[]{:S(2)}) async-start(), calls=%async_computation.13 | async-start | bytes 4915200 | tf_op jit(solution)/shard_map/all_gather | solution.py:15
  221.6 10.6 %copy-start.14 = (f32[1280]{0:T(1024)S(1)}, f32[1280]{0:T(1024)}, u32[]{:S(2)}) copy-start(f32[1280]{0:T(1024)} %param.28) | copy-start | bytes 15364
  231.3 101.5 %all-gather.4.cloned.1.call-start = ((), (), s32[]{:S(2)}) async-start(), calls=%async_computation.6 | async-start | bytes 5406720 | tf_op jit(solution)/shard_map/all_gather | solution.py:86
  231.9 176.0 %reduce-scatter.17.cloned.1.call-start = ((), (), s32[]{:S(2)}) async-start(), calls=%async_computation.12 | async-start | bytes 1228800 | tf_op jit(solution)/shard_map/reduce_scatter | solution.py:148
  271.5 2.8 copy-start.3
  271.5 2.8 copy-start.4
  274.3 2.0 copy-start.13
  275.6 4.0 copy-start.8
  283.1 156.8 %reduce-scatter.19.cloned.1.call-start = ((), (), s32[]{:S(2)}) async-start(), calls=%async_computation.14 | async-start | bytes 3686400
  290.0 1.2 copy-start.9
  290.0 1.9 copy-start.15
  290.0 229.0 %reduce-scatter.15.cloned.1.call-start = ((), (), s32[]{:S(2)}) async-start(), calls=%async_computation.11 | async-start | bytes 3686400 | tf_op jit(solution)/shard_map/reduce_scatter | solution.py:142
  295.5 1.2 copy-start.5
  295.5 441.8 %reduce-scatter.11.cloned.1.call-start = ((), (), s32[]{:S(2)}) async-start(), calls=%async_computation.9 | async-start | bytes 14745600 | tf_op jit(solution)/shard_map/reduce_scatter | solution.py:105
  303.3 1.4 copy-start.7
  303.3 652.1 %reduce-scatter.13.cloned.1.call-start = ((), (), s32[]{:S(2)}) async-start(), calls=%async_computation.10 | async-start | bytes 14745600 | tf_op jit(solution)/shard_map/reduce_scatter | solution.py:108
  311.3 21.6 %copy-start.2 = (bf16[512,1024]{1,0:T(8,128)(2,1)S(1)}, bf16[512,1024]{1,0:T(8,128)(2,1)}, u32[]{:S(2)}) copy-start(bf16[512,1024]{1,0:T(8,128)(2,1)} %fusion.4) | copy-start | bytes 3145732
  357.9 10.9 %copy-start.11 = (f32[1280]{0:T(1024)S(1)}, f32[1280]{0:T(1024)}, u32[]{:S(2)}) copy-start(f32[1280]{0:T(1024)} %get-tuple-element.68) | copy-start | bytes 15364
  357.9 597.5 %copy-start.1 = (bf16[1280,1280]{1,0:T(8,128)(2,1)S(1)}, bf16[1280,1280]{1,0:T(8,128)(2,1)}, u32[]{:S(2)}) copy-start(bf16[1280,1280]{1,0:T(8,128)(2,1)} %param.27) | copy-start | bytes 9830404
  (2 other events, 2.0 us)
Sparse Core Ops, SparseCore 0:
  32.1 142.8 reduce-scatter.8
  177.4 34.9 all-reduce.2
  231.5 33.3 all-gather.5
  267.5 65.3 all-gather.3
  335.9 22.8 reduce-scatter.16
  362.8 77.0 reduce-scatter.18
  444.1 74.8 reduce-scatter.14
  523.2 214.1 reduce-scatter.10
  741.6 213.8 reduce-scatter.12
